TPU v7x, 256 devices: a whole 4x4x8 slice. The times are simulated.
256 devices in a mesh: seq: 16 (over z, x_lo), wr: 4 (over y), wc: 4 (over x_hi, core).
Axes of the slice: x: 4 (x_hi: 2, x_lo: 2; x = x_hi * 2 + x_lo), y: 4, z: 8, core: 2. Of those that a mesh axis runs over, the one named last changes fastest.
Arguments:
- tokens: bfloat16 [8192, 2048], P('seq', ('wr', 'wc')), may hold values from -6 to 6
- ln_gain: float32 [2, 2048], replicated, may hold values from 0.5 to 1.5
- w_branch: bfloat16 [2, 2048, 4096], P(None, None, ('wr', 'wc')), may hold values from -0.125 to 0.125
- w_outgate: bfloat16 [2, 2048, 4096], P(None, None, ('wr', 'wc')), may hold values from -0.125 to 0.125
- w_gates: bfloat16 [2, 2048, 8], replicated, may hold values from -0.125 to 0.125
- forget_bias: float32 [2, 4], replicated, may hold values from 3.2 to 11
- conv_weight: float32 [2, 4, 4096], P(None, None, ('wr', 'wc')), may hold values from -3 to 3
- conv_bias: float32 [2, 4096], P(None, ('wr', 'wc')), may hold values from -3 to 3
- w_query: float32 [2, 4, 4, 4, 256], P(None, 'wr'), may hold values from -3 to 3
- w_key: float32 [2, 4, 4, 4, 256], P(None, 'wr'), may hold values from -3 to 3
- w_value: float32 [2, 4, 4, 4, 256], P(None, 'wr', None, 'wc'), may hold values from -4 to 4
- skip_gain: float32 [2, 4096], P(None, ('wr', 'wc')), may hold values from 0.5 to 1.5
- norm_gain: float32 [2, 4096], P(None, ('wr', 'wc')), may hold values from 0.5 to 1.5
- w_down: bfloat16 [2, 4096, 2048], P(None, ('wr', 'wc')), may hold values from -0.125 to 0.125
- lengths: int32 [3], replicated, may hold values from 1 to 4096, 8192 in all
- request_prompt: int32 [32], P('seq'), may hold values from 0 to 2
Outputs:
- mixed: bfloat16 [8192, 2048], P('seq', ('wr', 'wc'))
- request_state: bfloat16 [2, 32, 4, 1024, 1024], P(None, 'seq', 'wr', None, 'wc')
- request_conv: bfloat16 [2, 32, 3, 4096], P(None, 'seq', None, ('wr', 'wc'))
Inputs may be any that keep to these rules, and one draw needn't show every extreme that they name: `lengths`: the 3 prompts lie end to end in order and fill all 8192 positions; the longest has exactly 4096 positions.
All inputs are finite; a program needn't handle non-finite values.
Results may differ from a plain program's by a relative error of at most 0.035.
Values may be sent and summed in bfloat16 or wider, within the bound.
A program may use at most 128 MiB of HBM per device.

v0:
```python
import jax
import jax.numpy as jnp
from jax import lax
from jax.sharding import PartitionSpec as P

HEADS = 4
CONV = 4
LAYERS = 2
PROMPTS = 3
EPSILON = 1e-05
GATE_CAP = 15.0
ROW_DIMS = (((0,), (0,)), ((), ()))
FEATURE_DIMS = (((1,), (1,)), ((), ()))


def shifted(value, axis, steps):
    count = lax.axis_size(axis)
    first, last = (max(0, -steps), min(count, count - steps))
    return lax.ppermute(value, axis, [(source, source + steps) for source in range(first, last)])


def entering_2(shard, axis, join, neutral):
    place = lax.axis_index(axis)
    gathered = jax.tree.map(
        lambda a, kind: lax.all_gather(a.astype(kind), axis), shard, (jnp.bfloat16, jnp.bfloat16)
    )
    state = jax.tree.map(lambda a, e: jnp.zeros_like(a) + jnp.asarray(e, a.dtype), shard, neutral)

    def one(step, state):
        return join(
            state,
            jax.tree.map(
                lambda a, own: lax.dynamic_index_in_dim(a, step, 0, False).astype(own.dtype),
                gathered,
                shard,
            ),
        )

    return lax.fori_loop(0, place, one, state)


def broadcast(shard, axis, root):
    mine = lax.axis_index(axis) == root
    return lax.psum(jnp.where(mine, shard, jnp.zeros_like(shard)), axis)


def norm_rows(source, gain_row):
    widened = source.astype(jnp.float32)
    row_mean = jnp.mean(widened, axis=1, keepdims=True)
    row_var = jnp.mean(widened * widened, axis=1, keepdims=True) - row_mean * row_mean
    return ((widened - row_mean) * lax.rsqrt(row_var + EPSILON) * gain_row).astype(jnp.bfloat16)


def segment_of(positions, lengths):
    bound_one = lengths[0]
    bound_two = lengths[0] + lengths[1]
    return (positions >= bound_one).astype(jnp.int32) + (positions >= bound_two).astype(jnp.int32)


def conv_rows(extended, ext_segment, segment, weight, bias_row):
    row_count = segment.shape[0]
    widened = extended.astype(jnp.float32)
    summed = jnp.zeros((row_count, widened.shape[1]), jnp.float32) + bias_row
    for back_step in range(weight.shape[0]):
        low_row = weight.shape[0] - 1 - back_step
        keep_row = (ext_segment[low_row : low_row + row_count] == segment).astype(jnp.float32)
        summed = (
            summed + weight[back_step] * widened[low_row : low_row + row_count] * keep_row[:, None]
        )
    return jax.nn.silu(summed).astype(jnp.bfloat16)


def block_mix(source, weight):
    row_count = source.shape[0]
    grouped = source.astype(jnp.float32).reshape(row_count, 4, -1)
    mixed = jnp.einsum("tig,ijg->tjg", grouped, weight, precision=lax.Precision.HIGHEST)
    return mixed.reshape(row_count, -1)


def block_terms(queries, key_rows, values, log_forget, in_gate, segment, prev_seg):
    row_count = queries.shape[0]
    cum_log = jnp.cumsum(log_forget)
    row_order = jnp.arange(row_count)
    allowed = (row_order[:, None] >= row_order[None, :]) & (segment[:, None] == segment[None, :])
    exponent = jnp.where(allowed, cum_log[:, None] - cum_log[None, :] + in_gate[None, :], -jnp.inf)
    scores = lax.dot_general(
        queries, key_rows, FEATURE_DIMS, preferred_element_type=jnp.float32
    ) * jnp.exp(exponent)
    in_block = jnp.dot(scores.astype(jnp.bfloat16), values, preferred_element_type=jnp.float32)
    carried = jnp.where(segment == prev_seg, jnp.exp(cum_log), 0.0)
    last_seg = segment[row_count - 1]
    weights = jnp.where(
        segment == last_seg, jnp.exp(cum_log[row_count - 1] - cum_log + in_gate), 0.0
    )
    weighted = (key_rows.astype(jnp.float32) * weights[:, None]).astype(jnp.bfloat16)
    increment = lax.dot_general(weighted, values, ROW_DIMS, preferred_element_type=jnp.float32)
    block_decay = jnp.where(last_seg == prev_seg, jnp.exp(cum_log[row_count - 1]), 0.0)
    return (in_block, carried, increment, block_decay)


def end_state(
    state_in, key_rows, values, cum_log, in_gate, segment, seg_before, local_end, prompt, holder
):
    end_cum = cum_log[local_end]
    entering = jnp.where(holder & (seg_before == prompt), jnp.exp(end_cum), 0.0)
    row_order = jnp.arange(segment.shape[0])
    chosen = holder & (segment == prompt) & (row_order <= local_end)
    weights = jnp.where(chosen, jnp.exp(end_cum - cum_log + in_gate), 0.0)
    weighted = (key_rows.astype(jnp.float32) * weights[:, None]).astype(jnp.bfloat16)
    return entering * state_in + lax.dot_general(
        weighted, values, ROW_DIMS, preferred_element_type=jnp.float32
    )


def combine_states(earlier, later):
    return (earlier[0] * later[0], later[0] * earlier[1] + later[1])


def body(
    tokens,
    ln_gain,
    w_branch,
    w_outgate,
    w_gates,
    forget_bias,
    conv_weight,
    conv_bias,
    w_query,
    w_key,
    w_value,
    skip_gain,
    norm_gain,
    w_down,
    lengths,
    request_prompt,
):
    tok_rows = tokens.shape[0]
    seq_count = lax.axis_size("seq")
    seq_index = lax.axis_index("seq")
    head_idx = lax.axis_index("wr")
    row_offset = seq_index * tok_rows
    total_rows = tok_rows * seq_count
    row_ids = jnp.arange(tok_rows, dtype=jnp.int32)
    positions = row_offset + row_ids
    segment = segment_of(positions, lengths)
    seg_before = jnp.where(row_offset > 0, segment_of(row_offset - 1, lengths), -1)
    rim_positions = row_offset - (CONV - 1) + jnp.arange(CONV - 1, dtype=jnp.int32)
    rim_segment = jnp.where(rim_positions >= 0, segment_of(rim_positions, lengths), -1)
    ext_segment = jnp.concatenate([rim_segment, segment])
    prompt_starts = [jnp.zeros((), jnp.int32), lengths[0], lengths[0] + lengths[1]]
    prompt_ends = [
        lengths[0] - 1,
        lengths[0] + lengths[1] - 1,
        jnp.zeros((), jnp.int32) + (total_rows - 1),
    ]
    head_mask = (jnp.arange(HEADS, dtype=jnp.int32) == head_idx).astype(jnp.float32)
    current = tokens
    sent_states = []
    sent_edges = []
    for layer_idx in range(LAYERS):
        gathered = lax.all_gather(current, ("wr", "wc"), axis=1, tiled=True)
        normed = norm_rows(gathered, ln_gain[layer_idx])
        branch = jnp.dot(normed, w_branch[layer_idx], preferred_element_type=jnp.float32).astype(
            jnp.bfloat16
        )
        outgate = jnp.dot(normed, w_outgate[layer_idx], preferred_element_type=jnp.float32)
        gate_pre = jnp.dot(normed, w_gates[layer_idx], preferred_element_type=jnp.float32)
        input_pre = jnp.sum(gate_pre[:, :HEADS] * head_mask, axis=1)
        forget_pre = jnp.sum((gate_pre[:, HEADS:] + forget_bias[layer_idx]) * head_mask, axis=1)
        in_gate = GATE_CAP * jnp.tanh(input_pre / GATE_CAP)
        log_forget = jax.nn.log_sigmoid(forget_pre)
        edge_in = shifted(branch[tok_rows - (CONV - 1) :], "seq", 1)
        extended = jnp.concatenate([edge_in, branch], axis=0)
        conv_act = conv_rows(
            extended, ext_segment, segment, conv_weight[layer_idx], conv_bias[layer_idx]
        )
        head_branch, head_act = (
            lax.all_gather(branch, "wc", axis=1, tiled=True),
            lax.all_gather(conv_act, "wc", axis=1, tiled=True),
        )
        head_width = head_act.shape[1]
        queries = block_mix(head_act, w_query[layer_idx, 0]).astype(jnp.bfloat16)
        key_rows = (block_mix(head_act, w_key[layer_idx, 0]) * head_width ** (-0.5)).astype(
            jnp.bfloat16
        )
        values = block_mix(head_branch, w_value[layer_idx, 0]).astype(jnp.bfloat16)
        prefix = jnp.zeros((head_width, values.shape[1]), jnp.float32)
        reach_all = jnp.ones((), jnp.float32)
        in_block, carried, increment, block_decay = block_terms(
            queries, key_rows, values, log_forget, in_gate, segment, seg_before
        )
        saved_parts = (in_block, carried, reach_all, prefix)
        prefix = block_decay * prefix + increment
        reach_all = block_decay * reach_all
        entering = entering_2(
            (reach_all, prefix),
            "seq",
            combine_states,
            (jnp.ones((), jnp.float32), jnp.zeros_like(prefix)),
        )[1]
        in_block, carried, reach_here, prefix_here = saved_parts
        state_here = (reach_here * entering + prefix_here).astype(jnp.bfloat16)
        hidden_parts = in_block + carried[:, None] * jnp.dot(
            queries, state_here, preferred_element_type=jnp.float32
        )
        sums_one, sums_two = lax.psum(
            (jnp.sum(hidden_parts, axis=1), jnp.sum(hidden_parts * hidden_parts, axis=1)), "wc"
        )
        row_mean = sums_one / head_width
        row_var = sums_two / head_width - row_mean * row_mean
        normal_rows = (hidden_parts - row_mean[:, None]) * lax.rsqrt(row_var + EPSILON)[:, None]
        gated = (
            (
                normal_rows * norm_gain[layer_idx]
                + skip_gain[layer_idx] * conv_act.astype(jnp.float32)
            )
            * jax.nn.silu(outgate)
        ).astype(jnp.bfloat16)
        term_rows = jnp.dot(gated, w_down[layer_idx], preferred_element_type=jnp.float32)
        summed = lax.psum_scatter(
            term_rows.astype(jnp.bfloat16), ("wr", "wc"), scatter_dimension=1, tiled=True
        ).astype(jnp.float32)
        current = (current.astype(jnp.float32) + summed).astype(jnp.bfloat16)
        cum_log = jnp.cumsum(log_forget)
        for prompt in range(PROMPTS):
            end_pos = prompt_ends[prompt]
            holder = (end_pos >= row_offset) & (end_pos < row_offset + tok_rows)
            local_end = jnp.clip(end_pos - row_offset, 0, tok_rows - 1)
            state_end = end_state(
                entering,
                key_rows,
                values,
                cum_log,
                in_gate,
                segment,
                seg_before,
                local_end,
                prompt,
                holder,
            )
            window = lax.dynamic_slice_in_dim(extended, local_end + 1, CONV - 1, 0)
            edge_pos = end_pos - (CONV - 2) + jnp.arange(CONV - 1, dtype=jnp.int32)
            edge_rows = jnp.where(
                ((edge_pos >= prompt_starts[prompt]) & holder)[:, None],
                window,
                jnp.zeros_like(window),
            )
            got_state, got_edge = (
                broadcast(state_end.astype(jnp.bfloat16), "seq", end_pos // tok_rows),
                broadcast(edge_rows, "seq", end_pos // tok_rows),
            )
            sent_states.append(got_state)
            sent_edges.append(got_edge)
    state_stack = jnp.stack(sent_states)
    edge_stack = jnp.stack(sent_edges)
    state_stack = state_stack.reshape(LAYERS, PROMPTS, state_stack.shape[1], state_stack.shape[2])
    edge_stack = edge_stack.reshape(LAYERS, PROMPTS, edge_stack.shape[1], edge_stack.shape[2])
    chooser = (request_prompt[:, None] == jnp.arange(PROMPTS, dtype=jnp.int32)[None, :]).astype(
        jnp.bfloat16
    )
    request_state = jnp.einsum(
        "rp,lphd->lrhd", chooser, state_stack, preferred_element_type=jnp.float32
    ).astype(jnp.bfloat16)[:, :, None]
    request_conv = jnp.einsum(
        "rp,lpkc->lrkc", chooser, edge_stack, preferred_element_type=jnp.float32
    ).astype(jnp.bfloat16)
    return (current, request_state, request_conv)


def solution(mesh):
    return jax.shard_map(
        body,
        mesh=mesh,
        in_specs=(
            P("seq", ("wr", "wc")),
            P(),
            P(None, None, ("wr", "wc")),
            P(None, None, ("wr", "wc")),
            P(),
            P(),
            P(None, None, ("wr", "wc")),
            P(None, ("wr", "wc")),
            P(None, "wr", None, None, None),
            P(None, "wr", None, None, None),
            P(None, "wr", None, "wc", None),
            P(None, ("wr", "wc")),
            P(None, ("wr", "wc")),
            P(None, ("wr", "wc"), None),
            P(),
            P("seq"),
        ),
        out_specs=(
            P("seq", ("wr", "wc")),
            P(None, "seq", "wr", None, "wc"),
            P(None, "seq", None, ("wr", "wc")),
        ),
        check_vma=False,
    )
```

profile of v0, /device:TPU:8, one launch (start us, length us, event | category | flops | bytes accessed | tf_op | source)
XLA Modules:
  0.0 1085.9 jit_solution(4009449505985787538)
XLA Ops:
  17.0 47.1 %all-gather.11.cloned.1.call-done = bf16[512,2048]{1,0:T(8,128)(2,1)} async-done(((bf16[512,128]{1,0:T(8,128)(2,1)}), bf16[512,2048]{1,0:T(8,128)(2,1)}) %all-gather.11.cloned.1.call-update) | async-done | bytes 2097168 | tf_op jit(solution)/shard_map/all_gather | solution.py:161
  83.8 8.9 all-gather.15.cloned.1.call-done
  97.7 19.7 %all-gather.13.cloned.1.call-done = bf16[512,1024]{1,0:T(8,128)(2,1)} async-done(((bf16[512,256]{1,0:T(8,128)(2,1)}), bf16[512,1024]{1,0:T(8,128)(2,1)}) %all-gather.13.cloned.1.call-update) | async-done | bytes 1048592 | tf_op jit(solution)/shard_map/all_gather | solution.py:179
  122.8 4.2 fusion.99
  127.0 2.9 copy.92
  129.9 3.2 fusion.16
  144.2 38.1 %all-reduce = bf16[16]{0:T(256)(128)(2,1)S(1)} all-reduce(bf16[16]{0:T(256)(128)(2,1)} %dynamic-update-slice), channel_id=1, replica_groups=mesh['seq'=16,'wr'=4,'wc'=4] {'seq'}, use_global_device_ids=true, to_apply=%add | all-reduce | flops 16 | bytes 64
  182.3 2.9 fusion.26
  187.8 3.2 fusion.53
  191.0 130.3 %all-gather.23.cloned.1.call-done = bf16[16384,256]{1,0:T(8,128)(2,1)} async-done(((bf16[1024,256]{1,0:T(8,128)(2,1)}), bf16[16384,256]{1,0:T(8,128)(2,1)}) %all-gather.23.cloned.1.call-update) | async-done | bytes 8388624 | tf_op jit(solution)/shard_map/all_gather | solution.py:25
  324.8 9.4 all-reduce.3
  334.9 5.5 convolution_convert_fusion.1
  340.4 3.9 copy.136
  344.4 114.9 %reduce-scatter.7.cloned.1.call-done = bf16[128,512]{1,0:T(8,128)(2,1)} async-done(((bf16[2048,512]{1,0:T(8,128)(2,1)}), bf16[128,512]{1,0:T(8,128)(2,1)}) %reduce-scatter.7.cloned.1.call-update) | async-done | bytes 131088
  461.1 51.2 %all-gather.17.cloned.1.call-done = bf16[512,2048]{1,0:T(8,128)(2,1)} async-done(((bf16[512,128]{1,0:T(8,128)(2,1)}), bf16[512,2048]{1,0:T(8,128)(2,1)}) %all-gather.17.cloned.1.call-update) | async-done | bytes 2097168 | tf_op jit(solution)/shard_map/all_gather | solution.py:161
  529.3 3.2 exponential_select_fusion.1
  532.5 8.4 all-gather.21.cloned.1.call-done
  545.0 20.6 %all-gather.19.cloned.1.call-done = bf16[512,1024]{1,0:T(8,128)(2,1)} async-done(((bf16[512,256]{1,0:T(8,128)(2,1)}), bf16[512,1024]{1,0:T(8,128)(2,1)}) %all-gather.19.cloned.1.call-update) | async-done | bytes 1048592 | tf_op jit(solution)/shard_map/all_gather | solution.py:179
  568.9 4.2 fusion.96
  573.1 2.9 copy.102
  576.0 2.8 fusion.23
  590.7 71.5 %all-reduce.4 = (bf16[16]{0:T(256)(128)(2,1)S(1)}, bf16[1,3,256]{2,1,0:T(4,128)(2,1)S(1)}, bf16[1,3,256]{2,1,0:T(4,128)(2,1)S(1)}, bf16[1,3,256]{2,1,0:T(4,128)(...) all-reduce(bf16[16]{0:T(256)(128)(2,1)S(1)} %dynamic-update-slice.1, ...), channel_id=1, replica_groups=mesh['seq'=16,'wr'=4,'wc'=4] {'seq'}, use_global_device_ids=true, to_apply=%add.1 | all-reduce | flops 4624 | bytes 18496
  662.2 2.9 fusion.27
  667.5 3.3 fusion.52
  670.8 99.3 %all-gather.25.cloned.1.call-done = bf16[16384,256]{1,0:T(8,128)(2,1)} async-done(((bf16[1024,256]{1,0:T(8,128)(2,1)}), bf16[16384,256]{1,0:T(8,128)(2,1)}) %all-gather.25.cloned.1.call-update) | async-done | bytes 8388624 | tf_op jit(solution)/shard_map/all_gather | solution.py:25
  773.1 8.8 all-reduce.2
  782.0 6.1 convolution_convert_fusion
  788.1 3.9 copy.138
  798.1 3.4 fusion.19
  823.8 82.0 %reduce-scatter.9.cloned.1.call-done = bf16[128,512]{1,0:T(8,128)(2,1)} async-done(((bf16[2048,512]{1,0:T(8,128)(2,1)}), bf16[128,512]{1,0:T(8,128)(2,1)}) %reduce-scatter.9.cloned.1.call-update) | async-done | bytes 131088
  907.5 164.3 %all-reduce.8.cloned.1.call-done = (bf16[1,1024,256]{2,1,0:T(8,128)(2,1)}, bf16[1,1024,256]{2,1,0:T(8,128)(2,1)}, bf16[1,1024,256]{2,1,0:T(8,128)(2,1)}, bf16[1,...) async-done(((bf16[1,1024,256]{2,1,0:T(8,128)(2,1)}, bf16[1,1024,256]{2,1,0:T(8,128)(2,1)}, bf16[1,1024,256]{2,1,0:T(8,128)(2,1)}, ...) | async-done | bytes 3145744 | tf_op jit(solution)/shard_map/psum | solution.py:44
  1074.4 3.1 fusion.13
  (246 shorter events, 125.1 us)
Async XLA Ops:
  7.2 56.9 %all-gather.11.cloned.1.call-start = ((), (), s32[]{:S(2)}) async-start(), calls=%async_computation.2 | async-start | bytes 2228224 | tf_op jit(solution)/shard_map/all_gather | solution.py:161
  7.9 84.8 %all-gather.15.cloned.1.call-start = ((), (), s32[]{:S(2)}) async-start(), calls=%async_computation.4 | async-start | bytes 1310720 | tf_op jit(solution)/shard_map/all_gather | solution.py:178
  11.3 59.7 %copy-start.39 = (f32[4]{0:T(128)}, f32[4]{0:T(128)S(1)}, u32[]{:S(2)}) copy-start(f32[4]{0:T(128)S(1)} %compare_convert_fusion) | copy-start | bytes 52
  69.6 6.1 copy-start.15
  69.6 47.8 %all-gather.13.cloned.1.call-start = ((), (), s32[]{:S(2)}) async-start(), calls=%async_computation.3 | async-start | bytes 1310720 | tf_op jit(solution)/shard_map/all_gather | solution.py:179
  71.0 6.7 copy-start.29
  71.0 7.3 copy-start.23
  71.1 10.8 copy-start.24
  71.5 4.1 collective-permute-start
  75.5 8.3 copy-start.30
  75.7 8.1 copy-start.27
  76.9 244.4 %all-gather.23.cloned.1.call-start = ((), (), s32[]{:S(2)}) async-start(), calls=%async_computation.8 | async-start | bytes 8912896 | tf_op jit(solution)/shard_map/all_gather | solution.py:25
  133.1 5.5 copy-start.41
  133.2 6.1 copy-start.42
  138.0 321.3 %reduce-scatter.7.cloned.1.call-start = ((), (), s32[]{:S(2)}) async-start(), calls=%async_computation.10 | async-start | bytes 2228224
  344.3 116.0 %copy-start.17 = (bf16[512,128]{1,0:T(8,128)(2,1)S(1)}, bf16[512,128]{1,0:T(8,128)(2,1)}, u32[]{:S(2)}) copy-start(bf16[512,128]{1,0:T(8,128)(2,1)} %param.20) | copy-start | bytes 393220
  344.3 168.0 %all-gather.17.cloned.1.call-start = ((), (), s32[]{:S(2)}) async-start(), calls=%async_computation.5 | async-start | bytes 2228224 | tf_op jit(solution)/shard_map/all_gather | solution.py:161
  461.0 79.9 %all-gather.21.cloned.1.call-start = ((), (), s32[]{:S(2)}) async-start(), calls=%async_computation.7 | async-start | bytes 1310720 | tf_op jit(solution)/shard_map/all_gather | solution.py:178
  516.4 10.1 copy-start
  516.4 7.0 copy-start.34
  516.4 7.0 copy-start.35
  516.4 7.0 copy-start.36
  516.4 7.0 copy-start.37
  517.8 7.6 copy-start.26
  517.8 47.8 %all-gather.19.cloned.1.call-start = ((), (), s32[]{:S(2)}) async-start(), calls=%async_computation.6 | async-start | bytes 1310720 | tf_op jit(solution)/shard_map/all_gather | solution.py:179
  518.6 3.8 collective-permute-start.1
  525.2 244.9 %all-gather.25.cloned.1.call-start = ((), (), s32[]{:S(2)}) async-start(), calls=%async_computation.9 | async-start | bytes 8912896 | tf_op jit(solution)/shard_map/all_gather | solution.py:25
  585.6 320.2 %reduce-scatter.9.cloned.1.call-start = ((), (), s32[]{:S(2)}) async-start(), calls=%async_computation.11 | async-start | bytes 2228224
  770.4 11.5 %copy-start.44 = (f32[1,256]{1,0:T(1,128)S(1)}, f32[1,256]{1,0:T(1,128)}, u32[]{:S(2)}) copy-start(f32[1,256]{1,0:T(1,128)} %get-tuple-element.222) | copy-start | bytes 3076
  770.4 11.5 %copy-start.45 = (f32[1,256]{1,0:T(1,128)S(1)}, f32[1,256]{1,0:T(1,128)}, u32[]{:S(2)}) copy-start(f32[1,256]{1,0:T(1,128)} %get-tuple-element.220) | copy-start | bytes 3076
  792.0 279.8 %all-reduce.8.cloned.1.call-start = ((), (), s32[]{:S(2)}) async-start(), calls=%async_computation.12 | async-start | bytes 6291456 | tf_op jit(solution)/shard_map/psum | solution.py:44
  822.3 84.5 %copy-start.16 = (bf16[512,128]{1,0:T(8,128)(2,1)S(1)}, bf16[512,128]{1,0:T(8,128)(2,1)}, u32[]{:S(2)}) copy-start(bf16[512,128]{1,0:T(8,128)(2,1)} %add_convert_fusion.1) | copy-start | bytes 393220
  (31 other events, 73.3 us)
Sparse Core Ops, SparseCore 0:
  10.6 53.4 all-gather.10
  69.7 22.9 all-gather.14
  94.5 22.8 all-gather.12
  138.1 183.1 all-gather.22
  344.4 114.8 reduce-scatter.6
  462.3 49.9 all-gather.16
  518.0 22.8 all-gather.20
  542.7 22.8 all-gather.18
  585.7 184.3 all-gather.24
  792.1 113.6 reduce-scatter.8
  908.9 162.8 all-reduce.7
where the time goes:
time: 1100 us; the launch traced here: 1090 us
  waiting for transfers between devices  749 us (68%)
  blocking collectives  128 us (12%)
  local copies, waits for them, and re-layouts  79.5 us (7%)
  matrix products  59.7 us (5%)
  other arithmetic  39.7 us (4%)
  between operations  24.4 us (2%)
    all_gather x2, waiting for transfers between devices, entering_2(): lax.all_gather(a.astype(kind), axis)  230 us
    unnamed x13, waiting for transfers between devices  198 us
    psum x1, waiting for transfers between devices, broadcast(): return lax.psum(jnp.where(mine, shard, jnp.zeros_like(shard)), axis)  164 us
    unnamed x2, blocking collectives  110 us
    all_gather x2, waiting for transfers between devices, body(): gathered = lax.all_gather(current, ('wr', 'wc'), axis=1, tiled=True)  98.3 us
    all_gather x2, waiting for transfers between devices, body(): lax.all_gather(conv_act, 'wc', axis=1, tiled=True)  40.3 us
    unnamed x126, local copies, waits for them, and re-layouts  27.7 us
  transfers between devices with their start and end apart: 13, of which 12 were waited for; matrix products, arithmetic and copies ran while one was open for 8% of the time, Pallas kernels for 0%

commit v1 on v0

--- a/solution.py
+++ b/solution.py
@@ -41,7 +41,11 @@
 
 def broadcast(shard, axis, root):
     mine = lax.axis_index(axis) == root
-    return lax.psum(jnp.where(mine, shard, jnp.zeros_like(shard)), axis)
+
+    def _expand_columns(target):
+        return jnp.sum(jax.lax.all_gather(target, axis_name=axis), axis=0)
+
+    return _expand_columns(jnp.where(mine, shard, jnp.zeros_like(shard)))
 
 
 def norm_rows(source, gain_row):

time: 1100 us -> 2000 us (1.82)
  waiting for transfers between devices: 749 us -> 1420 us
  blocking collectives: 128 us -> 328 us
  other arithmetic: 39.7 us -> 66.7 us
    all_gather x0 -> x6, waiting for transfers between devices: none -> 825 us  [_expand_columns(): return jnp.sum(jax.lax.all_gather(target, axis_name=axis), axis=0)]
    all_gather x0 -> x6, blocking collectives: none -> 236 us  [_expand_columns(): return jnp.sum(jax.lax.all_gather(target, axis_name=axis), axis=0)]
    psum x1 -> x0, waiting for transfers between devices: 164 us -> none  [broadcast(): return lax.psum(jnp.where(mine, shard, jnp.zeros_like(shard)), axis)]
    unnamed x2, blocking collectives: 110 us -> 73.9 us
    reduce_sum x0 -> x12, other arithmetic: none -> 29.2 us  [_expand_columns(): return jnp.sum(jax.lax.all_gather(target, axis_name=axis), axis=0)]
    unnamed x13 -> x18, waiting for transfers between devices: 198 us -> 192 us
  transfers between devices with their start and end apart: 13 -> 18, of which waited for: 12 -> 16; matrix products, arithmetic and copies ran while one was open for 8% -> 6% of each run, Pallas kernels for 0% -> 0%
where the time goes in v1:
time: 2000 us; the launch traced here: 1990 us
  waiting for transfers between devices  1420 us (71%)
  blocking collectives  328 us (16%)
  local copies, waits for them, and re-layouts  75 us (4%)
  other arithmetic  66.7 us (3%)
  matrix products  62 us (3%)
  between operations  24.5 us (1%)
    all_gather x6, waiting for transfers between devices, _expand_columns(): return jnp.sum(jax.lax.all_gather(target, axis_name=axis), axis=0)  825 us
    all_gather x2, waiting for transfers between devices, entering_2(): lax.all_gather(a.astype(kind), axis)  249 us
    all_gather x6, blocking collectives, _expand_columns(): return jnp.sum(jax.lax.all_gather(target, axis_name=axis), axis=0)  236 us
    unnamed x18, waiting for transfers between devices  192 us
    all_gather x2, waiting for transfers between devices, body(): gathered = lax.all_gather(current, ('wr', 'wc'), axis=1, tiled=True)  98.4 us
    unnamed x2, blocking collectives  73.9 us
    all_gather x2, waiting for transfers between devices, body(): lax.all_gather(conv_act, 'wc', axis=1, tiled=True)  40.3 us
  transfers between devices with their start and end apart: 18, of which 16 were waited for; matrix products, arithmetic and copies ran while one was open for 6% of the time, Pallas kernels for 0%

profile of v1, /device:TPU:8, one launch (start us, length us, event | category | flops | bytes accessed | tf_op | source)
XLA Modules:
  0.0 1985.9 jit_solution(12658136994103058370)
XLA Ops:
  16.9 47.1 %all-gather.35.cloned.1.call-done = bf16[512,2048]{1,0:T(8,128)(2,1)} async-done(((bf16[512,128]{1,0:T(8,128)(2,1)}), bf16[512,2048]{1,0:T(8,128)(2,1)}) %all-gather.35.cloned.1.call-update) | async-done | bytes 2097168 | tf_op jit(solution)/shard_map/all_gather | solution.py:165
  83.7 8.9 all-gather.39.cloned.1.call-done
  97.7 19.7 all-gather.37.cloned.1.call-done
  144.0 38.8 %all-reduce = bf16[16]{0:T(256)(128)(2,1)S(1)} all-reduce(bf16[16]{0:T(256)(128)(2,1)} %dynamic-update-slice), channel_id=1, replica_groups=mesh['seq'=16,'wr'=4,'wc'=4] {'seq'}, use_global_device_ids=true, to_apply=%add | all-reduce | flops 16 | bytes 64
  191.5 129.7 %all-gather.47.cloned.1.call-done = bf16[16384,256]{1,0:T(8,128)(2,1)} async-done(((bf16[1024,256]{1,0:T(8,128)(2,1)}), bf16[16384,256]{1,0:T(8,128)(2,1)}) %all-gather.47.cloned.1.call-update) | async-done | bytes 8388624 | tf_op jit(solution)/shard_map/all_gather | solution.py:25
  324.7 9.4 all-reduce.3
  334.8 5.5 convolution_convert_fusion.1
  344.3 115.0 %reduce-scatter.7.cloned.1.call-done = bf16[128,512]{1,0:T(8,128)(2,1)} async-done(((bf16[2048,512]{1,0:T(8,128)(2,1)}), bf16[128,512]{1,0:T(8,128)(2,1)}) %reduce-scatter.7.cloned.1.call-update) | async-done | bytes 131088
  461.1 51.2 %all-gather.41.cloned.1.call-done = bf16[512,2048]{1,0:T(8,128)(2,1)} async-done(((bf16[512,128]{1,0:T(8,128)(2,1)}), bf16[512,2048]{1,0:T(8,128)(2,1)}) %all-gather.41.cloned.1.call-update) | async-done | bytes 2097168 | tf_op jit(solution)/shard_map/all_gather | solution.py:165
  532.4 8.5 all-gather.45.cloned.1.call-done
  545.1 20.6 %all-gather.43.cloned.1.call-done = bf16[512,1024]{1,0:T(8,128)(2,1)} async-done(((bf16[512,256]{1,0:T(8,128)(2,1)}), bf16[512,1024]{1,0:T(8,128)(2,1)}) %all-gather.43.cloned.1.call-update) | async-done | bytes 1048592 | tf_op jit(solution)/shard_map/all_gather | solution.py:183
  606.9 35.1 %all-reduce.1 = bf16[16]{0:T(256)(128)(2,1)S(1)} all-reduce(bf16[16]{0:T(256)(128)(2,1)S(1)} %dynamic-update-slice.1), channel_id=1, replica_groups=mesh['seq'=16,'wr'=4,'wc'=4] {'seq'}, use_global_device_ids=true, to_apply=%add.1 | all-reduce | flops 16 | bytes 64
  648.2 119.6 %all-gather.49.cloned.1.call-done = bf16[16384,256]{1,0:T(8,128)(2,1)} async-done(((bf16[1024,256]{1,0:T(8,128)(2,1)}), bf16[16384,256]{1,0:T(8,128)(2,1)}) %all-gather.49.cloned.1.call-update) | async-done | bytes 8388624 | tf_op jit(solution)/shard_map/all_gather | solution.py:25
  770.8 9.0 all-reduce.2
  779.8 5.5 convolution_convert_fusion
  799.0 74.7 %all-gather.16 = bf16[16,3,256]{2,1,0:T(4,128)(2,1)S(1)} all-gather(bf16[1,3,256]{2,1,0:T(4,128)(2,1)S(1)} %get-tuple-element.166), channel_id=12, replica_groups=mesh['seq'=16,'wr'=4,'wc'=4] {'seq'}, dimensions={0}, use_global_device_ids=true | all-gather | bytes 26112 | tf_op jit(solution)/shard_map/all_gather | solution.py:46
  873.7 30.4 %all-gather.14 = bf16[16,3,256]{2,1,0:T(4,128)(2,1)S(1)} all-gather(bf16[1,3,256]{2,1,0:T(4,128)(2,1)S(1)} %get-tuple-element.167), channel_id=10, replica_groups=mesh['seq'=16,'wr'=4,'wc'=4] {'seq'}, dimensions={0}, use_global_device_ids=true | all-gather | bytes 26112 | tf_op jit(solution)/shard_map/all_gather | solution.py:46
  904.2 34.5 %all-gather.15 = bf16[16,3,256]{2,1,0:T(4,128)(2,1)S(1)} all-gather(bf16[1,3,256]{2,1,0:T(4,128)(2,1)S(1)} %get-tuple-element.168), channel_id=11, replica_groups=mesh['seq'=16,'wr'=4,'wc'=4] {'seq'}, dimensions={0}, use_global_device_ids=true | all-gather | bytes 26112 | tf_op jit(solution)/shard_map/all_gather | solution.py:46
  938.9 30.0 %all-gather.19 = bf16[16,3,256]{2,1,0:T(4,128)(2,1)S(1)} all-gather(bf16[1,3,256]{2,1,0:T(4,128)(2,1)S(1)} %get-tuple-element.163), channel_id=15, replica_groups=mesh['seq'=16,'wr'=4,'wc'=4] {'seq'}, dimensions={0}, use_global_device_ids=true | all-gather | bytes 26112 | tf_op jit(solution)/shard_map/all_gather | solution.py:46
  968.9 36.1 %all-gather.17 = bf16[16,3,256]{2,1,0:T(4,128)(2,1)S(1)} all-gather(bf16[1,3,256]{2,1,0:T(4,128)(2,1)S(1)} %get-tuple-element.164), channel_id=13, replica_groups=mesh['seq'=16,'wr'=4,'wc'=4] {'seq'}, dimensions={0}, use_global_device_ids=true | all-gather | bytes 26112 | tf_op jit(solution)/shard_map/all_gather | solution.py:46
  1005.0 30.4 %all-gather.18 = bf16[16,3,256]{2,1,0:T(4,128)(2,1)S(1)} all-gather(bf16[1,3,256]{2,1,0:T(4,128)(2,1)S(1)} %get-tuple-element.165), channel_id=14, replica_groups=mesh['seq'=16,'wr'=4,'wc'=4] {'seq'}, dimensions={0}, use_global_device_ids=true | all-gather | bytes 26112 | tf_op jit(solution)/shard_map/all_gather | solution.py:46
  1036.3 4.8 reduce_sum.266
  1041.1 101.3 %all-gather.53.cloned.1.call-done = bf16[16384,256]{1,0:T(8,128)(2,1)} async-done(((bf16[1024,256]{1,0:T(8,128)(2,1)}), bf16[16384,256]{1,0:T(8,128)(2,1)}) %all-gather.53.cloned.1.call-update) | async-done | bytes 8388624 | tf_op jit(solution)/shard_map/all_gather | solution.py:46
  1142.5 4.8 reduce_sum.265
  1147.3 180.6 %all-gather.51.cloned.1.call-done = bf16[16384,256]{1,0:T(8,128)(2,1)} async-done(((bf16[1024,256]{1,0:T(8,128)(2,1)}), bf16[16384,256]{1,0:T(8,128)(2,1)}) %all-gather.51.cloned.1.call-update) | async-done | bytes 8388624 | tf_op jit(solution)/shard_map/all_gather | solution.py:46
  1327.9 4.8 reduce_sum.264
  1335.3 76.1 %reduce-scatter.9.cloned.1.call-done = bf16[128,512]{1,0:T(8,128)(2,1)} async-done(((bf16[2048,512]{1,0:T(8,128)(2,1)}), bf16[128,512]{1,0:T(8,128)(2,1)}) %reduce-scatter.9.cloned.1.call-update) | async-done | bytes 131088
  1413.1 181.7 %all-gather.61.cloned.1.call-done = bf16[16384,256]{1,0:T(8,128)(2,1)} async-done(((bf16[1024,256]{1,0:T(8,128)(2,1)}), bf16[16384,256]{1,0:T(8,128)(2,1)}) %all-gather.61.cloned.1.call-update) | async-done | bytes 8388624 | tf_op jit(solution)/shard_map/all_gather | solution.py:46
  1594.9 4.8 reduce_sum.269
  1599.7 180.7 %all-gather.57.cloned.1.call-done = bf16[16384,256]{1,0:T(8,128)(2,1)} async-done(((bf16[1024,256]{1,0:T(8,128)(2,1)}), bf16[16384,256]{1,0:T(8,128)(2,1)}) %all-gather.57.cloned.1.call-update) | async-done | bytes 8388624 | tf_op jit(solution)/shard_map/all_gather | solution.py:46
  1780.4 4.8 reduce_sum.267
  1785.2 180.2 %all-gather.59.cloned.1.call-done = bf16[16384,256]{1,0:T(8,128)(2,1)} async-done(((bf16[1024,256]{1,0:T(8,128)(2,1)}), bf16[16384,256]{1,0:T(8,128)(2,1)}) %all-gather.59.cloned.1.call-update) | async-done | bytes 8388624 | tf_op jit(solution)/shard_map/all_gather | solution.py:46
  (269 shorter events, 176.6 us)
Async XLA Ops:
  7.2 56.9 %all-gather.35.cloned.1.call-start = ((), (), s32[]{:S(2)}) async-start(), calls=%async_computation.2 | async-start | bytes 2228224 | tf_op jit(solution)/shard_map/all_gather | solution.py:165
  7.9 84.8 %all-gather.39.cloned.1.call-start = ((), (), s32[]{:S(2)}) async-start(), calls=%async_computation.4 | async-start | bytes 1310720 | tf_op jit(solution)/shard_map/all_gather | solution.py:182
  11.3 59.7 %copy-start.34 = (f32[4]{0:T(128)}, f32[4]{0:T(128)S(1)}, u32[]{:S(2)}) copy-start(f32[4]{0:T(128)S(1)} %compare_convert_fusion) | copy-start | bytes 52
  69.6 47.8 %all-gather.37.cloned.1.call-start = ((), (), s32[]{:S(2)}) async-start(), calls=%async_computation.3 | async-start | bytes 1310720 | tf_op jit(solution)/shard_map/all_gather | solution.py:183
  71.0 7.2 copy-start.18
  71.1 10.8 copy-start.19
  71.5 4.1 collective-permute-start
  75.5 19.0 copy-start.25
  75.7 18.9 copy-start.22
  76.9 244.4 %all-gather.47.cloned.1.call-start = ((), (), s32[]{:S(2)}) async-start(), calls=%async_computation.8 | async-start | bytes 8912896 | tf_op jit(solution)/shard_map/all_gather | solution.py:25
  138.0 321.3 %reduce-scatter.7.cloned.1.call-start = ((), (), s32[]{:S(2)}) async-start(), calls=%async_computation.16 | async-start | bytes 2228224
  344.2 116.1 %copy-start.16 = (bf16[512,128]{1,0:T(8,128)(2,1)S(1)}, bf16[512,128]{1,0:T(8,128)(2,1)}, u32[]{:S(2)}) copy-start(bf16[512,128]{1,0:T(8,128)(2,1)} %param.20) | copy-start | bytes 393220
  344.3 168.1 %all-gather.41.cloned.1.call-start = ((), (), s32[]{:S(2)}) async-start(), calls=%async_computation.5 | async-start | bytes 2228224 | tf_op jit(solution)/shard_map/all_gather | solution.py:165
  461.1 79.9 %all-gather.45.cloned.1.call-start = ((), (), s32[]{:S(2)}) async-start(), calls=%async_computation.7 | async-start | bytes 1310720 | tf_op jit(solution)/shard_map/all_gather | solution.py:182
  516.4 10.2 copy-start
  517.9 7.7 copy-start.21
  517.9 47.8 %all-gather.43.cloned.1.call-start = ((), (), s32[]{:S(2)}) async-start(), calls=%async_computation.6 | async-start | bytes 1310720 | tf_op jit(solution)/shard_map/all_gather | solution.py:183
  518.6 3.8 collective-permute-start.1
  525.3 242.6 %all-gather.49.cloned.1.call-start = ((), (), s32[]{:S(2)}) async-start(), calls=%async_computation.9 | async-start | bytes 8912896 | tf_op jit(solution)/shard_map/all_gather | solution.py:25
  584.5 451.8 %all-gather.55.cloned.1.call-start = ((), (), s32[]{:S(2)}) async-start(), calls=%async_computation.12 | async-start | bytes 8912896 | tf_op jit(solution)/shard_map/all_gather | solution.py:46
  594.9 547.6 %all-gather.53.cloned.1.call-start = ((), (), s32[]{:S(2)}) async-start(), calls=%async_computation.11 | async-start | bytes 8912896 | tf_op jit(solution)/shard_map/all_gather | solution.py:46
  600.5 727.5 %all-gather.51.cloned.1.call-start = ((), (), s32[]{:S(2)}) async-start(), calls=%async_computation.10 | async-start | bytes 8912896 | tf_op jit(solution)/shard_map/all_gather | solution.py:46
  605.1 806.3 %reduce-scatter.9.cloned.1.call-start = ((), (), s32[]{:S(2)}) async-start(), calls=%async_computation.17 | async-start | bytes 2228224
  768.0 11.8 copy-start.1
  768.0 11.8 copy-start.39
  768.0 11.8 copy-start.40
  789.2 805.7 %all-gather.61.cloned.1.call-start = ((), (), s32[]{:S(2)}) async-start(), calls=%async_computation.15 | async-start | bytes 8912896 | tf_op jit(solution)/shard_map/all_gather | solution.py:46
  792.3 988.2 %all-gather.57.cloned.1.call-start = ((), (), s32[]{:S(2)}) async-start(), calls=%async_computation.13 | async-start | bytes 8912896 | tf_op jit(solution)/shard_map/all_gather | solution.py:46
  794.8 1170.6 %all-gather.59.cloned.1.call-start = ((), (), s32[]{:S(2)}) async-start(), calls=%async_computation.14 | async-start | bytes 8912896 | tf_op jit(solution)/shard_map/all_gather | solution.py:46
  796.2 142.6 %copy-start.14 = (bf16[512,256]{1,0:T(8,128)(2,1)S(1)}, bf16[512,256]{1,0:T(8,128)(2,1)}, u32[]{:S(2)}) copy-start(bf16[512,256]{1,0:T(8,128)(2,1)} %convolution_convert_fusion.4) | copy-start | bytes 786436
  796.2 239.3 %copy-start.43 = (s32[2]{0:T(128)S(1)}, s32[2]{0:T(128)}, u32[]{:S(2)}) copy-start(s32[2]{0:T(128)} %param.35) | copy-start | bytes 28
  1332.8 79.6 %copy-start.15 = (bf16[512,128]{1,0:T(8,128)(2,1)S(1)}, bf16[512,128]{1,0:T(8,128)(2,1)}, u32[]{:S(2)}) copy-start(bf16[512,128]{1,0:T(8,128)(2,1)} %add_convert_fusion.1) | copy-start | bytes 393220
  (31 other events, 114.6 us)
Sparse Core Ops, SparseCore 0:
  10.6 53.4 all-gather.34
  69.7 22.9 all-gather.38
  94.5 22.8 all-gather.36
  138.1 183.1 all-gather.46
  344.4 114.8 reduce-scatter.6
  462.4 49.9 all-gather.40
  518.0 22.8 all-gather.44
  542.8 22.8 all-gather.42
  584.6 183.1 all-gather.48
  769.5 186.3 all-gather.54
  957.7 184.7 all-gather.52
  1144.1 183.7 all-gather.50
  1332.1 79.2 reduce-scatter.8
  1413.0 181.7 all-gather.60
  1597.1 183.2 all-gather.56
  1782.1 183.2 all-gather.58
